TPU v7x, 256 devices: a whole 4x4x8 slice. The times are simulated.
256 devices in a mesh: op: 16 (over x_lo, y, core), sec: 16 (over x_hi, z).
Axes of the slice: x: 4 (x_hi: 2, x_lo: 2; x = x_hi * 2 + x_lo), y: 4, z: 8, core: 2. Of those that a mesh axis runs over, the one named last changes fastest.
Arguments:
- psi: bfloat16 [16, 512, 512], P('sec'), may hold values from -6 to 6
- left_env: bfloat16 [128, 16, 512, 512], P('op', 'sec'), may hold values from -0.375 to 0.375
- right_env: bfloat16 [128, 16, 512, 512], P('op', 'sec'), may hold values from -0.25 to 0.25
- pair_code: int32 [128], P('op'), may hold values from 0 to 2
- sketch: bfloat16 [16, 512, 128], P('sec'), may hold values from -0.25 to 0.25
Outputs:
- sigma: bfloat16 [512, 8192], P('op', 'sec')
- basis: float32 [512, 2048], P('op', 'sec')
All inputs are finite; a program needn't handle non-finite values.
Results may differ from a plain program's by a relative error of at most 0.0055.
Values may be sent and summed in bfloat16 or wider, within the bound.
No kernel may reach another device: no remote copies, remote signals or barrier semaphores. Data moves between devices by JAX's collectives and lax.ppermute only.
A program may use at most 64 MiB of HBM per device.

v0:
```python
import math
import jax
import jax.numpy as jnp
from jax import lax
from jax.sharding import PartitionSpec as P


def padded_2(block, sides, width):
    for axis, dim in sides:
        count = lax.axis_size(axis)
        forward = [(i, i + 1) for i in range(count - 1)]
        backward = [(target, source) for source, target in forward]
        low = lax.ppermute(
            lax.slice_in_dim(block, block.shape[dim] - width, None, axis=dim), axis, forward
        )
        high = lax.ppermute(lax.slice_in_dim(block, 0, width, axis=dim), axis, backward)
        block = jnp.concatenate([low, block, high], axis=dim)
    return block


def range_basis(sigma_rows, sketch, width):
    count = sigma_rows.shape[0]
    sec_dev = sketch.shape[0]
    sampled = jnp.einsum(
        "ajd,jdk->jak",
        sigma_rows.reshape(count, sec_dev, width),
        sketch,
        preferred_element_type=jnp.float32,
    )
    return sampled


def finish_basis(sampled, gram, width):
    lower = jnp.linalg.cholesky(gram)
    solved = lax.linalg.triangular_solve(
        lower, sampled, left_side=False, lower=True, transpose_a=True
    )
    sec_dev, count, cols = solved.shape
    return math.sqrt(width) * solved.transpose(1, 0, 2).reshape(count, sec_dev * cols)


def body(psi, left_env, right_env, pair_code, sketch):
    t_dev, sec_dev, width, unused = left_env.shape
    n_op = lax.axis_size("op")
    rows = width // n_op
    scale = 1.0 / math.sqrt(t_dev * n_op)
    padded = padded_2(psi, (("sec", 0),), 1)

    def one_term(index, total):
        code = pair_code[index]
        source = lax.dynamic_slice_in_dim(padded, 2 - code, sec_dev, 0)
        left_rows = left_env[index]
        inner = jnp.einsum(
            "jab,jbc->jac", left_rows, source, preferred_element_type=jnp.float32
        ).astype(jnp.bfloat16)
        return total + scale * jnp.einsum(
            "jac,jcd->jad", inner, right_env[index], preferred_element_type=jnp.float32
        )

    total = lax.fori_loop(
        0, t_dev, one_term, jnp.zeros((sec_dev, lax.axis_size("op") * rows, width), jnp.float32)
    )
    summed = lax.psum_scatter(
        total.transpose(1, 0, 2).reshape(lax.axis_size("op") * rows, sec_dev * width),
        "op",
        scatter_dimension=0,
        tiled=True,
    )
    sigma_rows = summed.astype(jnp.bfloat16)
    sampled = range_basis(sigma_rows, sketch, width)
    gram_part = jnp.einsum("jak,jal->jkl", sampled, sampled, precision=lax.Precision.HIGHEST)
    gram = lax.psum(gram_part, "op")
    basis = finish_basis(sampled, gram, width)
    return (sigma_rows, basis)


def solution(mesh):
    in_specs = (
        P("sec", None, None),
        P("op", "sec", None, None),
        P("op", "sec", None, None),
        P("op"),
        P("sec", None, None),
    )
    out_specs = (P("op", "sec"), P("op", "sec"))
    return jax.shard_map(body, mesh=mesh, in_specs=in_specs, out_specs=out_specs, check_vma=False)
```

profile of v0, /device:TPU:25, one launch (start us, length us, event | category | flops | bytes accessed | tf_op | source)
XLA Modules:
  0.0 275.1 jit_solution(13141491743284272402)
XLA Ops:
  7.2 3.6 %collective-permute-start = (bf16[1,512,512]{2,1,0:T(8,128)(2,1)}, bf16[1,512,512]{2,1,0:T(8,128)(2,1)S(1)}, u32[]{:S(2)}, u32[]{:S(2)}) collective-permute-start(bf16[1,512,512]{2,1,0:T(8,128)(2,1)} %param.7), channel_id=1, source_target_pairs={{0,1},{1,2},{2,3},{3,4},{4,5},{5,6},{6,7},{7,8},{8,9},{9,10},{10,1... | collective-permute-start | bytes 1572872 | tf_op jit(solution)/shard_map/ppermute | solution.py:13
  10.8 1.3 collective-permute-start.1
  12.1 9.6 %collective-permute-done = bf16[1,512,512]{2,1,0:T(8,128)(2,1)S(1)} collective-permute-done((bf16[1,512,512]{2,1,0:T(8,128)(2,1)}, bf16[1,512,512]{2,1,0:T(8,128)(2,1)S(1)}, u32[]{:S(2)}, u32[]{:S(2)}) %collective-permute-start) | collective-permute-done | bytes 524320 | tf_op jit(solution)/shard_map/ppermute | solution.py:13
  21.7 4.2 %collective-permute-done.1 = bf16[1,512,512]{2,1,0:T(8,128)(2,1)} collective-permute-done((bf16[1,512,512]{2,1,0:T(8,128)(2,1)}, bf16[1,512,512]{2,1,0:T(8,128)(2,1)}, u32[]{:S(2)}, u32[]{:S(2)}) %collective-permute-start.1) | collective-permute-done | bytes 524320 | tf_op jit(solution)/shard_map/ppermute | solution.py:16
  25.9 1.4 pad_maximum_fusion
  27.2 31.5 %while.16 = (s32[]{:T(128)}, f32[1,512,512]{2,1,0:T(8,128)S(1)}, bf16[8,1,512,512]{3,2,1,0:T(8,128)(2,1)}, s32[8]{0:T(128)S(1)}, bf16[3,512,512]{2,1,0:T(8,128)(...) while((s32[]{:T(128)}, f32[1,512,512]{2,1,0:T(8,128)S(1)}, ...), condition=%wide.region_1.0_spmd.clone, body=%wide.region_0.0_spmd.clone.sunk | while | flops 537919488 | bytes 3671213 | solution.py:60
  27.3 0.6 dynamic_slice.65
  29.1 2.0 fusion.30
  31.2 0.6 dynamic_slice.65
  33.1 2.0 fusion.30
  35.1 0.6 dynamic_slice.65
  37.0 2.0 fusion.30
  39.1 0.6 dynamic_slice.65
  41.0 2.0 fusion.30
  43.0 0.6 dynamic_slice.65
  44.9 2.0 fusion.30
  48.8 2.0 fusion.30
  50.9 0.6 dynamic_slice.65
  52.8 2.0 fusion.30
  56.7 2.0 fusion.30
  58.8 1.0 copy-done.1
  59.8 66.4 %reduce-scatter.2.cloned.1.call-done = f32[32,512]{1,0:T(8,128)} async-done(((f32[512,512]{1,0:T(8,128)}), f32[32,512]{1,0:T(8,128)}) %reduce-scatter.2.cloned.1.call-update) | async-done | bytes 65552 | tf_op jit(solution)/shard_map/reduce_scatter | solution.py:63
  126.2 0.8 convert_element_type.14
  127.2 0.9 convolution_bitcast_fusion
  128.2 114.6 %all-reduce.2.cloned.1.call-done = f32[1,128,128]{1,2,0:T(8,128)} async-done(((f32[1,128,128]{1,2,0:T(8,128)}), f32[1,128,128]{1,2,0:T(8,128)}) %all-reduce.2.cloned.1.call-update) | async-done | bytes 65552 | tf_op jit(solution)/shard_map/psum | solution.py:72
  242.8 0.9 copy.8
  243.7 0.9 fusion.18
  244.6 11.7 %custom-call.7 = f32[1,128,128]{2,1,0:T(8,128)S(1)} custom-call(f32[1,128,128]{2,1,0:T(8,128)S(1)} %fusion.18), custom_call_target="Cholesky" | custom-call | tf_op jit(solution)/shard_map/jit(cholesky)/cholesky | solution.py:34
  256.3 0.6 compare_reduce_fusion
  256.9 0.7 fusion.16
  257.6 9.8 %custom-call.8 = f32[1,1,128,128]{2,3,1,0:T(8,128)S(1)} custom-call(f32[1,1,128,128]{3,2,1,0:T(8,128)S(1)} %fusion.16), custom_call_target="InvertDiagBlocksLowerTriangular" | custom-call | tf_op jit(solution)/shard_map/triangular_solve | solution.py:35
  267.4 0.8 convolution_multiply_fusion.1
  (16 shorter events, 1.5 us)
Async XLA Ops:
  7.2 119.9 %copy-start = (bf16[1,512,128]{2,1,0:T(8,128)(2,1)S(1)}, bf16[1,512,128]{2,1,0:T(8,128)(2,1)}, u32[]{:S(2)}) copy-start(bf16[1,512,128]{2,1,0:T(8,128)(2,1)} %param.11) | copy-start | bytes 393220
  7.2 119.1 %reduce-scatter.2.cloned.1.call-start = ((), (), s32[]{:S(2)}) async-start(), calls=%async_computation.1 | async-start | bytes 1114112 | tf_op jit(solution)/shard_map/reduce_scatter | solution.py:63
  7.2 14.5 %collective-permute-start = (bf16[1,512,512]{2,1,0:T(8,128)(2,1)}, bf16[1,512,512]{2,1,0:T(8,128)(2,1)S(1)}, u32[]{:S(2)}, u32[]{:S(2)}) collective-permute-start(bf16[1,512,512]{2,1,0:T(8,128)(2,1)} %param.7), channel_id=1, source_target_pairs={{0,1},{1,2},{2,3},{3,4},{4,5},{5,6},{6,7},{7,8},{8,9},{9,10},{10,1... | collective-permute-start | bytes 1572872 | tf_op jit(solution)/shard_map/ppermute | solution.py:13
  10.8 15.1 %collective-permute-start.1 = (bf16[1,512,512]{2,1,0:T(8,128)(2,1)}, bf16[1,512,512]{2,1,0:T(8,128)(2,1)}, u32[]{:S(2)}, u32[]{:S(2)}) collective-permute-start(bf16[1,512,512]{2,1,0:T(8,128)(2,1)} %param.7), channel_id=1, source_target_pairs={{1,0},{2,1},{3,2},{4,3},{5,4},{6,5},{7,6},{8,7},{9,8},{10,9},{11,1... | collective-permute-start | bytes 1572872 | tf_op jit(solution)/shard_map/ppermute | solution.py:16
  12.1 15.1 %copy-start.3 = (s32[8]{0:T(128)S(1)}, s32[8]{0:T(128)}, u32[]{:S(2)}) copy-start(s32[8]{0:T(128)} %param.10) | copy-start | bytes 100
  58.7 1.0 copy-start.1
  59.7 183.0 %all-reduce.2.cloned.1.call-start = ((), (), s32[]{:S(2)}) async-start(), calls=%async_computation.2 | async-start | bytes 131072 | tf_op jit(solution)/shard_map/psum | solution.py:72
  127.1 141.1 %copy-start.2 = (bf16[32,512]{1,0:T(8,128)(2,1)}, bf16[32,512]{1,0:T(8,128)(2,1)S(1)}, u32[]{:S(2)}) copy-start(bf16[32,512]{1,0:T(8,128)(2,1)S(1)} %convert_element_type.14) | copy-start | bytes 98308
Sparse Core Ops, SparseCore 0:
  59.9 66.3 reduce-scatter.1
  128.9 113.8 all-reduce.1
where the time goes:
time: 276 us; the launch traced here: 275 us
  waiting for transfers between devices  195 us (71%)
  other arithmetic  25.9 us (9%)
  matrix products  18 us (7%)
  between operations  14.1 us (5%)
  loops' own time  10.6 us (4%)
  local copies, waits for them, and re-layouts  6.61 us (2%)
  starting transfers between devices  4.95 us (2%)
    psum x1, waiting for transfers between devices, body(): gram = lax.psum(gram_part, 'op')  115 us
    reduce_scatter x1, waiting for transfers between devices, body(): lax.psum_scatter(total.transpose(1, 0, 2).reshape(lax.axis_size('op') * r...  66.4 us
    dot_general x8, matrix products, one_term(): jnp.einsum('jac,jcd->jad', inner, right_env[index], preferred_element_typ...  16.2 us
    another operation x3, other arithmetic, finish_basis(): lower = jnp.linalg.cholesky(gram)  12.4 us
    another operation x1, loops' own time, body(): lax.fori_loop(0, t_dev, one_term, jnp.zeros((sec_dev, lax.axis_size('op')...  10.6 us
    another operation x2, other arithmetic, finish_basis(): lax.linalg.triangular_solve(lower, sampled, left_side=False, lower=True,...  10.5 us
    ppermute x1, waiting for transfers between devices, padded_2(): lax.ppermute(lax.slice_in_dim(block, block.shape[dim] - width, None, axis...  9.55 us
  transfers between devices with their start and end apart: 4, of which 4 were waited for; matrix products, arithmetic and copies ran while one was open for 0% of the time, Pallas kernels for 0%

commit v1 on v0

--- a/solution.py
+++ b/solution.py
@@ -69,7 +69,8 @@
     sigma_rows = summed.astype(jnp.bfloat16)
     sampled = range_basis(sigma_rows, sketch, width)
     gram_part = jnp.einsum("jak,jal->jkl", sampled, sampled, precision=lax.Precision.HIGHEST)
-    gram = lax.psum(gram_part, "op")
+    parts = lax.all_gather(gram_part, "op")
+    gram = jnp.sum(parts, axis=0)
     basis = finish_basis(sampled, gram, width)
     return (sigma_rows, basis)
 

time: 276 us -> 197 us (0.71)
  waiting for transfers between devices: 195 us -> 115 us
    psum x1 -> x0, waiting for transfers between devices: 115 us -> none  [body(): gram = lax.psum(gram_part, 'op')]
    all_gather x0 -> x1, waiting for transfers between devices: none -> 34.5 us  [body(): parts = lax.all_gather(gram_part, 'op')]
where the time goes in v1:
time: 197 us; the launch traced here: 195 us
  waiting for transfers between devices  115 us (58%)
  other arithmetic  26.4 us (13%)
  matrix products  18 us (9%)
  between operations  14.2 us (7%)
  loops' own time  10.6 us (5%)
  local copies, waits for them, and re-layouts  5.86 us (3%)
  starting transfers between devices  4.95 us (3%)
    reduce_scatter x1, waiting for transfers between devices, body(): lax.psum_scatter(total.transpose(1, 0, 2).reshape(lax.axis_size('op') * r...  66.4 us
    all_gather x1, waiting for transfers between devices, body(): parts = lax.all_gather(gram_part, 'op')  34.5 us
    dot_general x8, matrix products, one_term(): jnp.einsum('jac,jcd->jad', inner, right_env[index], preferred_element_typ...  16.2 us
    another operation x3, other arithmetic, finish_basis(): lower = jnp.linalg.cholesky(gram)  12.4 us
    another operation x1, loops' own time, body(): lax.fori_loop(0, t_dev, one_term, jnp.zeros((sec_dev, lax.axis_size('op')...  10.6 us
    another operation x2, other arithmetic, finish_basis(): lax.linalg.triangular_solve(lower, sampled, left_side=False, lower=True,...  10.5 us
    ppermute x1, waiting for transfers between devices, padded_2(): lax.ppermute(lax.slice_in_dim(block, block.shape[dim] - width, None, axis...  9.55 us
    dynamic_slice x8, local copies, waits for them, and re-layouts, one_term(): code = pair_code[index]  4.69 us
  transfers between devices with their start and end apart: 4, of which 4 were waited for; matrix products, arithmetic and copies ran while one was open for 0% of the time, Pallas kernels for 0%

profile of v1, /device:TPU:25, one launch (start us, length us, event | category | flops | bytes accessed | tf_op | source)
XLA Modules:
  0.0 194.7 jit_solution(10923980764812404299)
XLA Ops:
  7.2 3.6 %collective-permute-start = (bf16[1,512,512]{2,1,0:T(8,128)(2,1)}, bf16[1,512,512]{2,1,0:T(8,128)(2,1)S(1)}, u32[]{:S(2)}, u32[]{:S(2)}) collective-permute-start(bf16[1,512,512]{2,1,0:T(8,128)(2,1)} %param.7), channel_id=1, source_target_pairs={{0,1},{1,2},{2,3},{3,4},{4,5},{5,6},{6,7},{7,8},{8,9},{9,10},{10,1... | collective-permute-start | bytes 1572872 | tf_op jit(solution)/shard_map/ppermute | solution.py:13
  10.8 1.3 collective-permute-start.1
  12.1 9.6 %collective-permute-done = bf16[1,512,512]{2,1,0:T(8,128)(2,1)S(1)} collective-permute-done((bf16[1,512,512]{2,1,0:T(8,128)(2,1)}, bf16[1,512,512]{2,1,0:T(8,128)(2,1)S(1)}, u32[]{:S(2)}, u32[]{:S(2)}) %collective-permute-start) | collective-permute-done | bytes 524320 | tf_op jit(solution)/shard_map/ppermute | solution.py:13
  21.7 4.2 %collective-permute-done.1 = bf16[1,512,512]{2,1,0:T(8,128)(2,1)} collective-permute-done((bf16[1,512,512]{2,1,0:T(8,128)(2,1)}, bf16[1,512,512]{2,1,0:T(8,128)(2,1)}, u32[]{:S(2)}, u32[]{:S(2)}) %collective-permute-start.1) | collective-permute-done | bytes 524320 | tf_op jit(solution)/shard_map/ppermute | solution.py:16
  25.9 1.4 pad_maximum_fusion
  27.2 31.5 %while.16 = (s32[]{:T(128)}, f32[1,512,512]{2,1,0:T(8,128)S(1)}, bf16[8,1,512,512]{3,2,1,0:T(8,128)(2,1)}, s32[8]{0:T(128)S(1)}, bf16[3,512,512]{2,1,0:T(8,128)(...) while((s32[]{:T(128)}, f32[1,512,512]{2,1,0:T(8,128)S(1)}, ...), condition=%wide.region_1.0_spmd.clone, body=%wide.region_0.0_spmd.clone.sunk | while | flops 537919488 | bytes 3671213 | solution.py:60
  27.3 0.6 dynamic_slice.65
  29.1 2.0 %fusion.31 = f32[1,512,512]{2,1,0:T(8,128)S(1)} fusion(f32[1,512,512]{2,1,0:T(8,128)S(1)} %get-tuple-element.238, bf16[8,1,512,512]{3,2,1,0:T(8,128)(2,1)} %get-tuple-element.252, s32[]{:T(128)} %get-tuple-element.237, bf16[3,512,512]{2,1,0:T(8,128)(2,1)S(1)} %get-tuple-element.251, s32[]{:T(128)S(6)} %select_n.30, ...), kind=kOutput, calls=%fused_computation.2.clone.1 | convolution fusion | flops 537919488 | bytes 3671045 | tf_op jit(solution)/shard_map/while/body/eval_jaxpr/jac,jcd->jad/dot_general | solution.py:56
  31.2 0.6 dynamic_slice.65
  33.1 2.0 %fusion.31 = f32[1,512,512]{2,1,0:T(8,128)S(1)} fusion(f32[1,512,512]{2,1,0:T(8,128)S(1)} %get-tuple-element.238, bf16[8,1,512,512]{3,2,1,0:T(8,128)(2,1)} %get-tuple-element.252, s32[]{:T(128)} %get-tuple-element.237, bf16[3,512,512]{2,1,0:T(8,128)(2,1)S(1)} %get-tuple-element.251, s32[]{:T(128)S(6)} %select_n.30, ...), kind=kOutput, calls=%fused_computation.2.clone.1 | convolution fusion | flops 537919488 | bytes 3671045 | tf_op jit(solution)/shard_map/while/body/eval_jaxpr/jac,jcd->jad/dot_general | solution.py:56
  35.1 0.6 dynamic_slice.65
  37.0 2.0 %fusion.31 = f32[1,512,512]{2,1,0:T(8,128)S(1)} fusion(f32[1,512,512]{2,1,0:T(8,128)S(1)} %get-tuple-element.238, bf16[8,1,512,512]{3,2,1,0:T(8,128)(2,1)} %get-tuple-element.252, s32[]{:T(128)} %get-tuple-element.237, bf16[3,512,512]{2,1,0:T(8,128)(2,1)S(1)} %get-tuple-element.251, s32[]{:T(128)S(6)} %select_n.30, ...), kind=kOutput, calls=%fused_computation.2.clone.1 | convolution fusion | flops 537919488 | bytes 3671045 | tf_op jit(solution)/shard_map/while/body/eval_jaxpr/jac,jcd->jad/dot_general | solution.py:56
  39.1 0.6 dynamic_slice.65
  41.0 2.0 %fusion.31 = f32[1,512,512]{2,1,0:T(8,128)S(1)} fusion(f32[1,512,512]{2,1,0:T(8,128)S(1)} %get-tuple-element.238, bf16[8,1,512,512]{3,2,1,0:T(8,128)(2,1)} %get-tuple-element.252, s32[]{:T(128)} %get-tuple-element.237, bf16[3,512,512]{2,1,0:T(8,128)(2,1)S(1)} %get-tuple-element.251, s32[]{:T(128)S(6)} %select_n.30, ...), kind=kOutput, calls=%fused_computation.2.clone.1 | convolution fusion | flops 537919488 | bytes 3671045 | tf_op jit(solution)/shard_map/while/body/eval_jaxpr/jac,jcd->jad/dot_general | solution.py:56
  43.0 0.6 dynamic_slice.65
  44.9 2.0 %fusion.31 = f32[1,512,512]{2,1,0:T(8,128)S(1)} fusion(f32[1,512,512]{2,1,0:T(8,128)S(1)} %get-tuple-element.238, bf16[8,1,512,512]{3,2,1,0:T(8,128)(2,1)} %get-tuple-element.252, s32[]{:T(128)} %get-tuple-element.237, bf16[3,512,512]{2,1,0:T(8,128)(2,1)S(1)} %get-tuple-element.251, s32[]{:T(128)S(6)} %select_n.30, ...), kind=kOutput, calls=%fused_computation.2.clone.1 | convolution fusion | flops 537919488 | bytes 3671045 | tf_op jit(solution)/shard_map/while/body/eval_jaxpr/jac,jcd->jad/dot_general | solution.py:56
  46.9 0.6 dynamic_slice.65
  48.8 2.0 %fusion.31 = f32[1,512,512]{2,1,0:T(8,128)S(1)} fusion(f32[1,512,512]{2,1,0:T(8,128)S(1)} %get-tuple-element.238, bf16[8,1,512,512]{3,2,1,0:T(8,128)(2,1)} %get-tuple-element.252, s32[]{:T(128)} %get-tuple-element.237, bf16[3,512,512]{2,1,0:T(8,128)(2,1)S(1)} %get-tuple-element.251, s32[]{:T(128)S(6)} %select_n.30, ...), kind=kOutput, calls=%fused_computation.2.clone.1 | convolution fusion | flops 537919488 | bytes 3671045 | tf_op jit(solution)/shard_map/while/body/eval_jaxpr/jac,jcd->jad/dot_general | solution.py:56
  50.9 0.6 dynamic_slice.65
  52.8 2.0 %fusion.31 = f32[1,512,512]{2,1,0:T(8,128)S(1)} fusion(f32[1,512,512]{2,1,0:T(8,128)S(1)} %get-tuple-element.238, bf16[8,1,512,512]{3,2,1,0:T(8,128)(2,1)} %get-tuple-element.252, s32[]{:T(128)} %get-tuple-element.237, bf16[3,512,512]{2,1,0:T(8,128)(2,1)S(1)} %get-tuple-element.251, s32[]{:T(128)S(6)} %select_n.30, ...), kind=kOutput, calls=%fused_computation.2.clone.1 | convolution fusion | flops 537919488 | bytes 3671045 | tf_op jit(solution)/shard_map/while/body/eval_jaxpr/jac,jcd->jad/dot_general | solution.py:56
  56.7 2.0 %fusion.31 = f32[1,512,512]{2,1,0:T(8,128)S(1)} fusion(f32[1,512,512]{2,1,0:T(8,128)S(1)} %get-tuple-element.238, bf16[8,1,512,512]{3,2,1,0:T(8,128)(2,1)} %get-tuple-element.252, s32[]{:T(128)} %get-tuple-element.237, bf16[3,512,512]{2,1,0:T(8,128)(2,1)S(1)} %get-tuple-element.251, s32[]{:T(128)S(6)} %select_n.30, ...), kind=kOutput, calls=%fused_computation.2.clone.1 | convolution fusion | flops 537919488 | bytes 3671045 | tf_op jit(solution)/shard_map/while/body/eval_jaxpr/jac,jcd->jad/dot_general | solution.py:56
  58.8 1.0 copy-done.1
  59.8 66.4 %reduce-scatter.2.cloned.1.call-done = f32[32,512]{1,0:T(8,128)} async-done(((f32[512,512]{1,0:T(8,128)}), f32[32,512]{1,0:T(8,128)}) %reduce-scatter.2.cloned.1.call-update) | async-done | bytes 65552 | tf_op jit(solution)/shard_map/reduce_scatter | solution.py:63
  126.2 0.8 convert_element_type.14
  127.2 0.9 fusion.19
  128.2 34.5 %all-gather.3.cloned.1.call-done = f32[2048,128]{1,0:T(8,128)} async-done(((f32[128,128]{1,0:T(8,128)}), f32[2048,128]{1,0:T(8,128)}) %all-gather.3.cloned.1.call-update) | async-done | bytes 1048592 | tf_op jit(solution)/shard_map/all_gather | solution.py:72
  162.7 1.3 reduce.10
  164.2 11.7 %custom-call.7 = f32[1,128,128]{2,1,0:T(8,128)S(1)} custom-call(f32[1,128,128]{2,1,0:T(8,128)S(1)} %fusion.17), custom_call_target="Cholesky" | custom-call | tf_op jit(solution)/shard_map/jit(cholesky)/cholesky | solution.py:34
  175.9 0.6 compare_reduce_fusion
  176.6 0.7 fusion.16
  177.3 9.8 %custom-call.8 = f32[1,1,128,128]{2,3,1,0:T(8,128)S(1)} custom-call(f32[1,1,128,128]{3,2,1,0:T(8,128)S(1)} %fusion.16), custom_call_target="InvertDiagBlocksLowerTriangular" | custom-call | tf_op jit(solution)/shard_map/triangular_solve | solution.py:35
  187.1 0.8 convolution_multiply_fusion.1
  (18 shorter events, 1.1 us)
Async XLA Ops:
  7.2 119.9 %copy-start = (bf16[1,512,128]{2,1,0:T(8,128)(2,1)S(1)}, bf16[1,512,128]{2,1,0:T(8,128)(2,1)}, u32[]{:S(2)}) copy-start(bf16[1,512,128]{2,1,0:T(8,128)(2,1)} %param.11) | copy-start | bytes 393220
  7.2 119.1 %reduce-scatter.2.cloned.1.call-start = ((), (), s32[]{:S(2)}) async-start(), calls=%async_computation.1 | async-start | bytes 1114112 | tf_op jit(solution)/shard_map/reduce_scatter | solution.py:63
  7.2 14.5 %collective-permute-start = (bf16[1,512,512]{2,1,0:T(8,128)(2,1)}, bf16[1,512,512]{2,1,0:T(8,128)(2,1)S(1)}, u32[]{:S(2)}, u32[]{:S(2)}) collective-permute-start(bf16[1,512,512]{2,1,0:T(8,128)(2,1)} %param.7), channel_id=1, source_target_pairs={{0,1},{1,2},{2,3},{3,4},{4,5},{5,6},{6,7},{7,8},{8,9},{9,10},{10,1... | collective-permute-start | bytes 1572872 | tf_op jit(solution)/shard_map/ppermute | solution.py:13
  10.8 15.1 %collective-permute-start.1 = (bf16[1,512,512]{2,1,0:T(8,128)(2,1)}, bf16[1,512,512]{2,1,0:T(8,128)(2,1)}, u32[]{:S(2)}, u32[]{:S(2)}) collective-permute-start(bf16[1,512,512]{2,1,0:T(8,128)(2,1)} %param.7), channel_id=1, source_target_pairs={{1,0},{2,1},{3,2},{4,3},{5,4},{6,5},{7,6},{8,7},{9,8},{10,9},{11,1... | collective-permute-start | bytes 1572872 | tf_op jit(solution)/shard_map/ppermute | solution.py:16
  12.1 15.1 %copy-start.3 = (s32[8]{0:T(128)S(1)}, s32[8]{0:T(128)}, u32[]{:S(2)}) copy-start(s32[8]{0:T(128)} %param.10) | copy-start | bytes 100
  58.7 1.0 copy-start.1
  59.7 103.0 %all-gather.3.cloned.1.call-start = ((), (), s32[]{:S(2)}) async-start(), calls=%async_computation.2 | async-start | bytes 1114112 | tf_op jit(solution)/shard_map/all_gather | solution.py:72
  127.1 60.8 %copy-start.2 = (bf16[32,512]{1,0:T(8,128)(2,1)}, bf16[32,512]{1,0:T(8,128)(2,1)S(1)}, u32[]{:S(2)}) copy-start(bf16[32,512]{1,0:T(8,128)(2,1)S(1)} %convert_element_type.14) | copy-start | bytes 98308
Sparse Core Ops, SparseCore 0:
  59.9 66.3 reduce-scatter.1
  128.3 34.3 all-gather.2
